TPU v7x, 32 devices: a whole 2x2x4 slice. The times are simulated.
32 devices in a mesh: groups: 1, fac: 32 (over z, y, x, core).
Axes of the slice: x: 2, y: 2, z: 4, core: 2. Of those that a mesh axis runs over, the one named last changes fastest.
Arguments:
- sky_image: float32 [64, 96, 4096], P(('groups', 'fac')), may hold values from 0 to 18, as said below
- measured_real: float32 [64, 96, 4096], P(('groups', 'fac')), may hold values from -6 to 6
- measured_imaginary: float32 [64, 96, 4096], P(('groups', 'fac')), may hold values from -6 to 6
- sampling_mask: int32 [64, 96, 4096], P(('groups', 'fac')), may hold values 0 or 1
- dual_field: float32 [64, 96, 4096], P('groups', None, 'fac'), may hold values from -6 to 6
Outputs:
- next_image: float32 [64, 96, 4096], P(('groups', 'fac'))
- next_dual: float32 [64, 96, 4096], P('groups', None, 'fac')
Inputs may be any that keep to these rules, and one draw needn't show every extreme that they name: `sky_image`: non-negative sky brightness.
All inputs are finite; a program needn't handle non-finite values. No bound on the sum of `sampling_mask` on one device may be relied on, other than what follows from the above.
Results may differ from a plain program's by a relative error of at most 0.00012.
Values sent between devices are 32-bit elements; how exact they have to be, the bound alone decides.
No kernel may reach another device: no remote copies, remote signals or barrier semaphores. Data moves between devices by JAX's collectives and lax.ppermute only.
A program may use at most 192 MiB of HBM per device.

v0:
```python
import jax
import jax.numpy as jnp
import numpy as np
from jax import lax
from jax.sharding import PartitionSpec as P

LEVELS = 4
low_pass = (
    0.2303778133088964,
    0.7148465705529155,
    0.6308807679298587,
    -0.0279837694168599,
    -0.1870348117190931,
    0.0308413818355607,
    0.0328830116668852,
    -0.010597401785069,
)
high_pass = tuple(((-1) ** tap_index * low_pass[7 - tap_index] for tap_index in range(8)))
primal_step = 0.6
dual_step = 0.8
ball_radius = 12.0
precise = lax.Precision.HIGHEST


def contract(pattern, left_side, right_side):
    return jnp.einsum(
        pattern, left_side, right_side, precision=precise, preferred_element_type=jnp.float32
    )


def fourier_table(length, direction):
    sample_grid = np.arange(length)
    angles = 2.0 * np.pi * (np.outer(sample_grid, sample_grid) % length) / length
    factor = 1.0 / np.sqrt(length)
    return (
        jnp.asarray(np.cos(angles) * factor, jnp.float32),
        jnp.asarray(direction * np.sin(angles) * factor, jnp.float32),
    )


def twist_table(inner_size, outer_size, length, direction):
    angles = (
        2.0
        * np.pi
        * (np.arange(inner_size)[:, None] * np.arange(outer_size)[None, :] % length)
        / length
    )
    return (
        jnp.asarray(np.cos(angles), jnp.float32),
        jnp.asarray(direction * np.sin(angles), jnp.float32),
    )


def complex_step(real_part, imag_part, pattern, matrix):
    if imag_part is None:
        return (contract(pattern, real_part, matrix[0]), contract(pattern, real_part, matrix[1]))
    return (
        contract(pattern, real_part, matrix[0]) - contract(pattern, imag_part, matrix[1]),
        contract(pattern, real_part, matrix[1]) + contract(pattern, imag_part, matrix[0]),
    )


def data_gradient(sky_image, measured_real, measured_imaginary, sampling_mask):
    channels, row_count, column_count = sky_image.shape
    outer_size = 64
    inner_size = column_count // outer_size
    sample_grid = sky_image.reshape(channels, row_count, inner_size, outer_size)
    real_part, imag_part = complex_step(
        sample_grid, None, "crba,rs->csba", fourier_table(row_count, -1.0)
    )
    real_part, imag_part = complex_step(
        real_part, imag_part, "csba,bk->cska", fourier_table(inner_size, -1.0)
    )
    twist_real, twist_imag = twist_table(inner_size, outer_size, column_count, -1.0)
    real_part, imag_part = (
        real_part * twist_real - imag_part * twist_imag,
        real_part * twist_imag + imag_part * twist_real,
    )
    real_part, imag_part = complex_step(
        real_part, imag_part, "cska,aj->csjk", fourier_table(outer_size, -1.0)
    )
    weights = sampling_mask.astype(jnp.float32)
    real_part = weights * (real_part.reshape(channels, row_count, column_count) - measured_real)
    imag_part = weights * (
        imag_part.reshape(channels, row_count, column_count) - measured_imaginary
    )
    real_part = real_part.reshape(channels, row_count, outer_size, inner_size)
    imag_part = imag_part.reshape(channels, row_count, outer_size, inner_size)
    real_part, imag_part = complex_step(
        real_part, imag_part, "csjk,ja->cska", fourier_table(outer_size, 1.0)
    )
    twist_real, twist_imag = twist_table(inner_size, outer_size, column_count, 1.0)
    real_part, imag_part = (
        real_part * twist_real - imag_part * twist_imag,
        real_part * twist_imag + imag_part * twist_real,
    )
    real_part, imag_part = complex_step(
        real_part, imag_part, "cska,kb->csba", fourier_table(inner_size, 1.0)
    )
    row_real, row_imag = fourier_table(row_count, 1.0)
    result = contract("csba,sr->crba", real_part, row_real) - contract(
        "csba,sr->crba", imag_part, row_imag
    )
    return result.reshape(channels, row_count, column_count)


def row_matrix(length):
    current = np.eye(length)
    details = []
    for level_index in range(LEVELS):
        width_now = current.shape[0]
        half_size = width_now // 2
        lower = np.zeros((half_size, width_now))
        upper = np.zeros((half_size, width_now))
        for target in range(half_size):
            for tap_index in range(8):
                lower[target, (2 * target + tap_index) % width_now] += low_pass[tap_index]
                upper[target, (2 * target + tap_index) % width_now] += high_pass[tap_index]
        details.insert(0, upper @ current)
        current = lower @ current
    return jnp.asarray(np.concatenate([current] + details, 0), jnp.float32)


def analysis_step(length):
    half_size = length // 2
    matrix = np.zeros((length + 6, length))
    for target in range(half_size):
        for tap_index in range(8):
            matrix[2 * target + tap_index, target] += low_pass[tap_index]
            matrix[2 * target + tap_index, half_size + target] += high_pass[tap_index]
    return jnp.asarray(matrix, jnp.float32)


def synthesis_step(length):
    matrix = np.zeros((2 * (length + 3), 2 * length))
    for source in range(length):
        for parity in range(2):
            for back_step in range(4):
                matrix[source - back_step + 3, 2 * source + parity] += low_pass[
                    parity + 2 * back_step
                ]
                matrix[length + 3 + source - back_step + 3, 2 * source + parity] += high_pass[
                    parity + 2 * back_step
                ]
    return jnp.asarray(matrix, jnp.float32)


def column_analysis(values, right_rim):
    coarse = values
    details = []
    for level_index in range(LEVELS):
        length = coarse.shape[-1]
        extended = jnp.concatenate([coarse, right_rim(coarse[..., :6])], -1)
        halves = contract("...m,mk->...k", extended, analysis_step(length))
        details.insert(0, halves[..., length // 2 :])
        coarse = halves[..., : length // 2]
    return jnp.concatenate([coarse] + details, -1)


def column_synthesis(coefficients, left_rim):
    length = coefficients.shape[-1] >> LEVELS
    coarse = coefficients[..., :length]
    offset = length
    for level_index in range(LEVELS):
        detail = coefficients[..., offset : offset + length]
        coarse_edge, detail_edge = left_rim(coarse[..., -3:], detail[..., -3:])
        extended = jnp.concatenate([coarse_edge, coarse, detail_edge, detail], -1)
        coarse = contract("...m,mk->...k", extended, synthesis_step(length))
        offset = offset + length
        length = length * 2
    return coarse


def right_within(edge_cols):
    return jnp.roll(edge_cols, -1, axis=-2)


def left_within(coarse_edge, detail_edge):
    return (jnp.roll(coarse_edge, 1, axis=-2), jnp.roll(detail_edge, 1, axis=-2))


def shards(sky_image, measured_real, measured_imaginary, sampling_mask, dual_field):
    channels, row_count, column_count = sky_image.shape
    rows_table = row_matrix(row_count)
    gradient = data_gradient(sky_image, measured_real, measured_imaginary, sampling_mask)
    facet_count = lax.axis_size("fac")
    facet_width = column_count // facet_count
    local_dual = lax.all_to_all(dual_field, "fac", split_axis=0, concat_axis=2, tiled=True)
    coefficients = local_dual.reshape(channels, row_count, facet_count, facet_width)
    prior_term = column_synthesis(coefficients, left_within).reshape(
        channels, row_count, column_count
    )
    prior_term = contract("sr,csn->crn", rows_table, prior_term)
    next_image = jnp.maximum(sky_image - primal_step * (gradient + prior_term), 0.0)
    analysed = contract("rs,csn->crn", rows_table, 2.0 * next_image - sky_image)
    analysed = column_analysis(
        analysed.reshape(channels, row_count, facet_count, facet_width), right_within
    )
    lifted = local_dual + dual_step * analysed.reshape(channels, row_count, column_count)
    summed = lax.psum(jnp.sum(lifted * lifted, axis=0), "fac")
    shrunk = lifted / jnp.maximum(1.0, jnp.sqrt(summed) / ball_radius)
    next_dual = lax.all_to_all(shrunk, "fac", split_axis=2, concat_axis=0, tiled=True)
    return (next_image, next_dual)


def solution(mesh):
    return jax.shard_map(
        shards,
        mesh=mesh,
        in_specs=(
            P(("groups", "fac"), None, None),
            P(("groups", "fac"), None, None),
            P(("groups", "fac"), None, None),
            P(("groups", "fac"), None, None),
            P("groups", None, "fac"),
        ),
        out_specs=(P(("groups", "fac"), None, None), P("groups", None, "fac")),
        check_vma=False,
    )
```

profile of v0, /device:TPU:0, one launch (start us, length us, event | category | flops | bytes accessed | tf_op | source)
XLA Modules:
  0.0 563.5 jit_solution(9362236796377634353)
XLA Ops:
  7.2 7.4 %all-to-all-start = ((f32[64,96,128]{2,1,0:T(8,128)}), f32[64,96,128]{2,1,0:T(8,128)}, u32[]{:S(2)}, u32[]{:S(2)}) async-start(f32[64,96,128]{2,1,0:T(8,128)} %param.34), calls=%async_computation | async-start | bytes 6291456 | tf_op jit(solution)/shard_map/all_to_all | solution.py:188
  14.7 3.3 copy.124
  18.0 5.8 %fusion.127 = f32[96,8192]{0,1:S(1)} fusion(f32[96,96]{1,0:T(8,128)S(1)} %copy-done.20, f32[96,8192]{0,1:T(8,128)} %bitcast.150), kind=kOutput, calls=%fused_computation.137 | convolution fusion | flops 905969664 | bytes 6328320
  23.8 3.6 fusion.126
  27.4 6.6 %fusion.37 = f32[2,96,64,64]{1,3,2,0:T(8,128)S(1)} fusion(f32[64,64,1,1]{0,1,3,2:T(8,128)S(1)} %copy-done.13, f32[2,96,64,64]{1,3,2,0:T(8,128)S(1)} %bitcast.154), kind=kOutput, calls=%fused_computation.56 | convolution fusion | flops 603979776 | bytes 6307840 | tf_op jit(solution)/shard_map/csba,bk->cska/dot_general | solution.py:26
  34.0 6.8 %fusion.35 = f32[2,96,64,64]{1,3,2,0:T(8,128)S(1)} fusion(f32[64,64,1,1]{0,1,3,2:T(8,128)S(1)} %copy-done.10, f32[2,96,64,64]{1,3,2,0:T(8,128)S(1)} %bitcast.155), kind=kOutput, calls=%fused_computation.54 | convolution fusion | flops 603979776 | bytes 6307840 | tf_op jit(solution)/shard_map/csba,bk->cska/dot_general | solution.py:26
  40.8 6.6 %fusion.60 = f32[2,96,64,64]{1,3,2,0:T(8,128)S(1)} fusion(f32[2,96,64,64]{1,3,2,0:T(8,128)S(1)} %fusion.37, f32[64,64,1,1]{0,1,3,2:T(8,128)S(1)} %copy-done.10, f32[2,96,64,64]{1,3,2,0:T(8,128)S(1)} %bitcast.152), kind=kOutput, calls=%fused_computation.80 | convolution fusion | flops 604766208 | bytes 9453568 | tf_op jit(solution)/shard_map/csba,bk->cska/dot_general | solution.py:26
  47.5 11.3 %fusion.13 = (f32[2,96,64,64]{1,2,3,0:T(8,128)}, f32[2,96,64,64]{1,2,3,0:T(8,128)S(1)}) fusion(f32[2,96,64,64]{1,3,2,0:T(8,128)S(1)} %fusion.60, f32[64,64]{0,1:T(8,128)S(1)} %copy-done.15, f32[64,64]{0,1:T(8,128)S(1)} %copy-done.9, f32[2,96,64,64]{1,3,2,0:T(8,128)S(1)} %fusion.35, f32[64,64,1,1]{0,1,3,2:T(8,128)S(1)} %copy-done.13, ...), kind=kOutput, calls=%fused_computation.20 | convolution fusion | flops 609484800 | bytes 15777792 | tf_op jit(solution)/shard_map/csba,bk->cska/dot_general | solution.py:26
  58.7 7.1 %fusion.29 = f32[2,96,64,64]{1,3,2,0:T(8,128)} fusion(f32[64,64,1,1]{0,1,3,2:T(8,128)S(1)} %copy-done.13, f32[2,96,64,64]{1,2,3,0:T(8,128)S(1)} %get-tuple-element.5), kind=kOutput, calls=%fused_computation.48 | convolution fusion | flops 603979776 | bytes 6307840 | tf_op jit(solution)/shard_map/cska,aj->csjk/dot_general | solution.py:26
  65.8 7.1 %fusion.27 = f32[2,96,64,64]{1,3,2,0:T(8,128)} fusion(f32[64,64,1,1]{0,1,3,2:T(8,128)S(1)} %copy-done.10, f32[2,96,64,64]{1,2,3,0:T(8,128)S(1)} %get-tuple-element.5), kind=kOutput, calls=%fused_computation.46 | convolution fusion | flops 603979776 | bytes 6307840 | tf_op jit(solution)/shard_map/cska,aj->csjk/dot_general | solution.py:26
  72.9 5.3 copy.132
  78.2 9.7 %subtract_bitcast_fusion.1 = f32[2,96,64,64]{1,2,3,0:T(8,128)S(1)} fusion(f32[2,96,64,64]{1,3,2,0:T(8,128)} %fusion.29, f32[64,64,1,1]{0,1,3,2:T(8,128)S(1)} %copy-done.10, f32[2,96,64,64]{1,2,3,0:T(8,128)} %get-tuple-element.4), kind=kOutput, calls=%fused_computation.37 | convolution fusion | flops 604766208 | bytes 9453568 | tf_op jit(solution)/shard_map/cska,aj->csjk/dot_general | solution.py:26
  87.8 4.4 copy.131
  92.2 5.1 copy.123
  97.4 5.3 copy.137
  102.7 9.7 %add_bitcast_fusion.1 = f32[2,96,64,64]{1,2,3,0:T(8,128)S(1)} fusion(f32[2,96,64,64]{1,3,2,0:T(8,128)} %fusion.27, f32[64,64,1,1]{0,1,3,2:T(8,128)S(1)} %copy-done.13, f32[2,96,64,64]{1,2,3,0:T(8,128)} %get-tuple-element.4), kind=kOutput, calls=%fused_computation.36 | convolution fusion | flops 604766208 | bytes 9453568 | tf_op jit(solution)/shard_map/cska,aj->csjk/dot_general | solution.py:26
  112.4 4.4 copy.136
  116.7 11.3 %fusion.12 = (f32[2,96,4096]{1,2,0:T(8,128)}, f32[2,96,4096]{1,2,0:T(8,128)}) fusion(f32[2,96,4096]{1,2,0:T(8,128)} %copy.132, f32[2,96,64,64]{1,3,2,0:T(8,128)} %copy.131, s32[2,96,4096]{1,2,0:T(8,128)} %copy.123, f32[2,96,4096]{1,2,0:T(8,128)} %copy.137, f32[2,96,64,64]{1,3,2,0:T(8,128)} %copy.136), kind=kLoop, calls=%fused_computation.17 | loop fusion | flops 3932160 | bytes 22020096 | tf_op jit(solution)/shard_map/mul | solution.py:83
  128.0 10.9 %fusion.19 = f32[2,96,64,64]{1,3,2,0:T(8,128)} fusion(f32[64,64,1,1]{0,1,3,2:T(8,128)S(1)} %copy-done.10, f32[2,96,64,64]{1,3,2,0:T(8,128)} %bitcast.164), kind=kOutput, calls=%fused_computation.38 | convolution fusion | flops 603979776 | bytes 6307840 | tf_op jit(solution)/shard_map/csjk,ja->cska/dot_general | solution.py:26
  138.9 7.1 %fusion.21 = f32[2,96,64,64]{1,3,2,0:T(8,128)} fusion(f32[64,64,1,1]{0,1,3,2:T(8,128)S(1)} %copy-done.12, f32[2,96,64,64]{1,3,2,0:T(8,128)S(1)} %bitcast.165), kind=kOutput, calls=%fused_computation.40 | convolution fusion | flops 603979776 | bytes 6307840 | tf_op jit(solution)/shard_map/csjk,ja->cska/dot_general | solution.py:26
  146.0 7.1 %fusion.23 = f32[2,96,64,64]{1,3,2,0:T(8,128)} fusion(f32[64,64,1,1]{0,1,3,2:T(8,128)S(1)} %copy-done.12, f32[2,96,64,64]{1,3,2,0:T(8,128)S(1)} %bitcast.162), kind=kOutput, calls=%fused_computation.42 | convolution fusion | flops 603979776 | bytes 6307840 | tf_op jit(solution)/shard_map/csjk,ja->cska/dot_general | solution.py:26
  153.1 7.2 %fusion.25 = f32[2,96,64,64]{1,3,2,0:T(8,128)} fusion(f32[64,64,1,1]{0,1,3,2:T(8,128)S(1)} %copy-done.10, f32[2,96,64,64]{1,3,2,0:T(8,128)S(1)} %bitcast.163), kind=kOutput, calls=%fused_computation.44 | convolution fusion | flops 603979776 | bytes 6307840 | tf_op jit(solution)/shard_map/csjk,ja->cska/dot_general | solution.py:26
  160.3 17.0 %copy_add_fusion = (f32[2,96,64,64]{1,2,3,0:T(8,128)S(1)}, f32[2,96,64,64]{1,2,3,0:T(8,128)}) fusion(f32[2,96,64,64]{1,3,2,0:T(8,128)} %fusion.19, f32[2,96,64,64]{1,3,2,0:T(8,128)} %fusion.23, f32[2,96,64,64]{1,3,2,0:T(8,128)} %fusion.21, f32[2,96,64,64]{1,3,2,0:T(8,128)} %fusion.25), kind=kLoop, calls=%fused_computation.29 | loop fusion | flops 1572864 | bytes 18874368 | tf_op jit(solution)/shard_map/add | solution.py:59
  177.3 6.7 %fusion.74 = f32[2,96,64,64]{1,3,2,0:T(8,128)S(1)} fusion(f32[64,64,1,1]{0,1,3,2:T(8,128)S(1)} %copy-done.12, f32[2,96,64,64]{1,2,3,0:T(8,128)S(1)} %get-tuple-element.26, f32[2,96,64,64]{1,2,3,0:T(8,128)} %get-tuple-element.27, f32[64,64]{0,1:T(8,128)S(1)} %copy-done.11, f32[64,64]{0,1:T(8,128)S(1)} %copy-done.9), kind=kOutput, calls=%fused_computation.85 | convolution fusion | flops 606339072 | bytes 9486336 | tf_op jit(solution)/shard_map/cska,kb->csba/dot_general | solution.py:26
  184.1 5.5 add_bitcast_fusion
  189.6 6.5 %fusion.15 = f32[2,64,64,96]{3,2,1,0:T(8,128)S(1)} fusion(f32[96,96,1,1]{1,0,3,2:T(8,128)S(1)} %copy-done.19, f32[2,96,64,64]{1,2,3,0:T(8,128)S(1)} %add_bitcast_fusion), kind=kOutput, calls=%fused_computation.25 | convolution fusion | flops 905969664 | bytes 6328320 | tf_op jit(solution)/shard_map/csba,sr->crba/dot_general | solution.py:26
  196.1 5.3 fusion.75
  201.5 5.3 subtract_bitcast_fusion
  206.8 7.4 %fusion.70 = f32[2,64,64,96]{3,2,1,0:T(8,128)} fusion(f32[2,64,64,96]{3,2,1,0:T(8,128)S(1)} %fusion.15, f32[96,96,1,1]{1,0,3,2:T(8,128)S(1)} %copy-done.18, f32[2,96,64,64]{1,2,3,0:T(8,128)S(1)} %subtract_bitcast_fusion), kind=kOutput, calls=%fused_computation.82 | convolution fusion | flops 906756096 | bytes 9474048 | tf_op jit(solution)/shard_map/csba,sr->crba/dot_general | solution.py:26
  214.2 5.3 copy.149
  219.5 5.2 copy.147
  224.7 1.9 slice.211
  230.3 2.5 fusion.48
  232.9 2.6 pad_maximum_fusion
  235.5 7.8 %copy.148 = f32[2,96,32,134]{3,2,1,0:T(8,128)} copy(f32[2,96,32,134]{1,3,2,0:T(8,128)} %pad_maximum_fusion) | data formatting | bytes 6586368 | tf_op jit(solution)/shard_map/concatenate | solution.py:167
  243.3 8.3 %fusion.128 = f32[2,96,32,128]{3,2,1,0:T(8,128)} fusion(f32[2,96,32,134]{3,2,1,0:T(8,128)} %copy.148, f32[134,128,1,1]{1,0,3,2:T(8,128)S(1)} %copy-done.17), kind=kOutput, calls=%fused_computation.138 | convolution fusion | flops 1264582656 | bytes 6507520 | tf_op jit(solution)/shard_map/...m,mk->...k/dot_general | solution.py:26
  251.6 4.9 reshape.48
  256.5 6.3 %fusion.9 = f32[2,96,4096]{2,1,0:T(8,128)S(1)} fusion(f32[2,96,4096]{2,1,0:T(8,128)S(1)} %copy-done.6, f32[2,96,4096]{2,1,0:T(8,128)} %copy.149, f32[2,96,4096]{2,1,0:T(8,128)} %reshape.48, f32[96,96,1]{0,1,2:T(8,128)S(1)} %copy-done.14), kind=kOutput, calls=%fused_computation.10 | convolution fusion | flops 909115392 | bytes 12619776 | tf_op jit(solution)/shard_map/sr,csn->crn/dot_general | solution.py:26
  262.9 3.3 fusion.45
  267.7 5.5 fusion
  276.0 8.4 %fusion.43 = f32[2,96,32,64]{1,3,2,0:T(8,128)S(1)} fusion(f32[70,64,1,1]{0,1,3,2:T(8,128)S(1)} %copy-done.22, f32[2,96,32,70]{3,2,1,0:T(8,128)S(1)} %maximum_maximum_fusion), kind=kOutput, calls=%fused_computation.63 | convolution fusion | flops 330301440 | bytes 3311104 | tf_op jit(solution)/shard_map/...m,mk->...k/dot_general | solution.py:26
  287.9 3.1 copy.170
  292.7 7.0 %multiply_reduce_fusion = (f32[96,32,128]{0,2,1:T(8,128)}, f32[2,96,32,128]{1,3,2,0:T(8,128)}) fusion(f32[2,96,32,64]{1,3,2,0:T(8,128)} %copy.170, f32[2,96,32,32]{1,3,2,0:T(8,128)} %get-tuple-element.23, f32[2,96,32,16]{1,3,2,0:T(8,128)} %get-tuple-element.25, f32[2,96,32,16]{1,3,2,0:T(8,128)S(1)} %fusion.106, f32[32,2,96,128]{2,3,0,1:T(8,128)} %copy.147), kind=kLoop, calls=%fused_computation.31 | loop fusion | flops 5111808 | bytes 11010048 | tf_op jit(solution)/shard_map/reduce_sum | solution.py:200
  299.6 135.1 %all-reduce.2.cloned.1.call-done = f32[96,4096]{0,1:T(8,128)} async-done(((f32[96,4096]{0,1:T(8,128)}), f32[96,4096]{0,1:T(8,128)}) %all-reduce.2.cloned.1.call-update) | async-done | bytes 1572880 | tf_op jit(solution)/shard_map/psum | solution.py:200
  434.7 2.4 multiply_maximum_fusion
  437.6 15.1 %copy_divide_fusion = f32[2,96,4096]{1,0,2:T(2,128)S(1)} fusion(f32[2,96,4096]{1,2,0:T(8,128)S(1)} %bitcast.169, f32[96,4096]{0,1:T(8,128)S(1)} %multiply_maximum_fusion), kind=kLoop, calls=%fused_computation.24 | loop fusion | flops 786432 | bytes 7864320 | tf_op jit(solution)/shard_map/div | solution.py:201
  452.7 97.1 %all_to_all.33 = f32[2,96,4096]{1,0,2:T(2,128)} all-to-all(f32[2,96,4096]{1,0,2:T(2,128)S(1)} %copy_divide_fusion), channel_id=1, replica_groups=mesh['groups'=1,'fac'=32] {'fac'}, dimensions={2} | all-to-all | bytes 6291456 | tf_op jit(solution)/shard_map/all_to_all | solution.py:202
  549.8 6.6 %copy.154 = f32[32,2,96,128]{3,2,1,0:T(8,128)} copy(f32[32,2,96,128]{2,1,3,0:T(2,128)} %bitcast.171) | data formatting | bytes 6291456 | tf_op jit(solution)/shard_map/all_to_all | solution.py:202
  (87 shorter events, 13.6 us)
Async XLA Ops:
  7.2 7.5 %copy-start.5 = (f32[2,96,4096]{2,1,0:T(8,128)S(1)}, f32[2,96,4096]{2,1,0:T(8,128)}, u32[]{:S(2)}) copy-start(f32[2,96,4096]{2,1,0:T(8,128)} %param.30) | copy-start | bytes 9437188
  7.2 212.3 %all-to-all-start = ((f32[64,96,128]{2,1,0:T(8,128)}), f32[64,96,128]{2,1,0:T(8,128)}, u32[]{:S(2)}, u32[]{:S(2)}) async-start(f32[64,96,128]{2,1,0:T(8,128)} %param.34), calls=%async_computation | async-start | bytes 6291456 | tf_op jit(solution)/shard_map/all_to_all | solution.py:188
  14.6 3.4 copy-start.20
  14.6 420.1 %all-reduce.2.cloned.1.call-start = ((), (), s32[]{:S(2)}) async-start(), calls=%async_computation.2 | async-start | bytes 4194304 | tf_op jit(solution)/shard_map/psum | solution.py:200
  18.0 5.8 %copy-start.1 = (f32[2,96,4096]{1,2,0:T(8,128)S(1)}, f32[2,96,4096]{1,2,0:T(8,128)}, u32[]{:S(2)}) copy-start(f32[2,96,4096]{1,2,0:T(8,128)} %copy.124) | copy-start | bytes 9437188
  18.0 5.8 %copy-start.21 = (f32[96,96]{1,0:T(8,128)S(1)}, f32[96,96]{1,0:T(8,128)}, u32[]{:S(2)}) copy-start(f32[96,96]{1,0:T(8,128)} %constant.51.clone) | copy-start | bytes 110596
  23.8 3.6 copy-start.13
  27.4 6.6 %copy-start.10 = (f32[64,64,1,1]{0,1,3,2:T(8,128)S(1)}, f32[64,64,1,1]{0,1,3,2:T(8,128)}, u32[]{:S(2)}) copy-start(f32[64,64,1,1]{0,1,3,2:T(8,128)} %constant.72) | copy-start | bytes 49156
  40.8 6.6 %copy-start.9 = (f32[64,64]{0,1:T(8,128)S(1)}, f32[64,64]{0,1:T(8,128)}, u32[]{:S(2)}) copy-start(f32[64,64]{0,1:T(8,128)} %constant.55.clone) | copy-start | bytes 49156
  40.8 6.6 %copy-start.15 = (f32[64,64]{0,1:T(8,128)S(1)}, f32[64,64]{0,1:T(8,128)}, u32[]{:S(2)}) copy-start(f32[64,64]{0,1:T(8,128)} %constant.56.clone) | copy-start | bytes 49156
  128.0 10.9 %copy-start.4 = (f32[2,96,4096]{1,2,0:T(8,128)S(1)}, f32[2,96,4096]{1,2,0:T(8,128)}, u32[]{:S(2)}) copy-start(f32[2,96,4096]{1,2,0:T(8,128)} %get-tuple-element.19) | copy-start | bytes 9437188
  128.0 10.9 %copy-start.12 = (f32[64,64,1,1]{0,1,3,2:T(8,128)S(1)}, f32[64,64,1,1]{0,1,3,2:T(8,128)}, u32[]{:S(2)}) copy-start(f32[64,64,1,1]{0,1,3,2:T(8,128)} %constant.74) | copy-start | bytes 49156
  138.9 7.1 %copy-start.3 = (f32[2,96,4096]{1,2,0:T(8,128)S(1)}, f32[2,96,4096]{1,2,0:T(8,128)}, u32[]{:S(2)}) copy-start(f32[2,96,4096]{1,2,0:T(8,128)} %get-tuple-element.18) | copy-start | bytes 9437188
  160.3 17.0 %copy-start.11 = (f32[64,64]{0,1:T(8,128)S(1)}, f32[64,64]{0,1:T(8,128)}, u32[]{:S(2)}) copy-start(f32[64,64]{0,1:T(8,128)} %constant.58.clone) | copy-start | bytes 49156
  177.3 6.7 %copy-start = (f32[2,96,64,64]{1,2,3,0:T(8,128)S(1)}, f32[2,96,64,64]{1,2,3,0:T(8,128)}, u32[]{:S(2)}) copy-start(f32[2,96,64,64]{1,2,3,0:T(8,128)} %get-tuple-element.27) | copy-start | bytes 9437188
  184.0 5.6 copy-start.19
  201.5 5.4 copy-start.18
  224.7 2.8 copy-start.2
  224.7 3.2 copy-start.27
  227.5 1.3 copy-start.26
  227.8 2.6 copy-start.25
  235.5 7.8 %copy-start.17 = (f32[134,128,1,1]{1,0,3,2:T(8,128)S(1)}, f32[134,128,1,1]{1,0,3,2:T(8,128)}, u32[]{:S(2)}) copy-start(f32[134,128,1,1]{1,0,3,2:T(8,128)} %constant.80) | copy-start | bytes 205828
  251.6 4.9 copy-start.6
  251.6 5.0 copy-start.14
  262.8 3.4 copy-start.8
  266.8 0.9 copy-start.16
  274.8 1.1 copy-start.22
  276.0 9.6 %copy-start.23 = (f32[38,32,1,1]{0,1,3,2:T(8,128)S(1)}, f32[38,32,1,1]{0,1,3,2:T(8,128)}, u32[]{:S(2)}) copy-start(f32[38,32,1,1]{0,1,3,2:T(8,128)} %constant.84) | copy-start | bytes 14596
  286.7 4.2 copy-start.24
  434.7 2.8 copy-start.7
Sparse Core Ops, SparseCore 0:
  299.8 134.9 all-reduce.1
where the time goes:
time: 567 us; the launch traced here: 563 us
  matrix products  183 us (32%)
  waiting for transfers between devices  135 us (24%)
  blocking collectives  97.1 us (17%)
  local copies, waits for them, and re-layouts  69.9 us (12%)
  other arithmetic  56.4 us (10%)
  between operations  14.9 us (3%)
  starting transfers between devices  7.46 us (1%)
    dot_general x28, matrix products, contract(): jnp.einsum(pattern, left_side, right_side, precision=precise, preferred_e...  173 us
    psum x1, waiting for transfers between devices, shards(): summed = lax.psum(jnp.sum(lifted * lifted, axis=0), 'fac')  135 us
    all_to_all x1, blocking collectives, shards(): lax.all_to_all(shrunk, 'fac', split_axis=2, concat_axis=0, tiled=True)  97.1 us
    unnamed x62, local copies, waits for them, and re-layouts  24.6 us
    add x1, other arithmetic, complex_step(): contract(pattern, real_part, matrix[1])  17 us
    div x1, other arithmetic, shards(): shrunk = lifted / jnp.maximum(1.0, jnp.sqrt(summed) / ball_radius)  15.1 us
  transfers between devices with their start and end apart: 2, of which 1 were waited for; matrix products, arithmetic and copies ran while one was open for 36% of the time, Pallas kernels for 0%

commit v1 on v0

--- a/solution.py
+++ b/solution.py
@@ -197,7 +197,7 @@
         analysed.reshape(channels, row_count, facet_count, facet_width), right_within
     )
     lifted = local_dual + dual_step * analysed.reshape(channels, row_count, column_count)
-    summed = lax.psum(jnp.sum(lifted * lifted, axis=0), "fac")
+    summed = jnp.sum(lax.all_gather(jnp.sum(lifted * lifted, axis=0), "fac"), axis=0)
     shrunk = lifted / jnp.maximum(1.0, jnp.sqrt(summed) / ball_radius)
     next_dual = lax.all_to_all(shrunk, "fac", split_axis=2, concat_axis=0, tiled=True)
     return (next_image, next_dual)

time: 567 us -> 718 us (1.27)
  waiting for transfers between devices: 135 us -> 277 us
  other arithmetic: 56.4 us -> 63.9 us
    all_gather x0 -> x1, waiting for transfers between devices: none -> 277 us  [shards(): lax.all_gather(jnp.sum(lifted * lifted, axis=0), 'fac')]
    psum x1 -> x0, waiting for transfers between devices: 135 us -> none  [shards(): summed = lax.psum(jnp.sum(lifted * lifted, axis=0), 'fac')]
    reduce_sum x1 -> x2, other arithmetic: 6.95 us -> 22.5 us  [the longest x1 16.9 us: shards(): jnp.sum(lax.all_gather(jnp.sum(lifted * lifted, axis=0), 'fac'), axis=0)]
    div x1, other arithmetic: 15.1 us -> 7.8 us  [shards(): shrunk = lifted / jnp.maximum(1.0, jnp.sqrt(summed) / ball_radius)]
    unnamed x62 -> x64, local copies, waits for them, and re-layouts: 24.6 us -> 23 us
  transfers between devices with their start and end apart: 2 -> 2, of which waited for: 1 -> 1; matrix products, arithmetic and copies ran while one was open for 36% -> 28% of each run, Pallas kernels for 0% -> 0%
where the time goes in v1:
time: 718 us; the launch traced here: 714 us
  waiting for transfers between devices  277 us (39%)
  matrix products  180 us (25%)
  blocking collectives  96.3 us (13%)
  local copies, waits for them, and re-layouts  74.8 us (10%)
  other arithmetic  63.9 us (9%)
  between operations  15 us (2%)
  starting transfers between devices  7.46 us (1%)
    all_gather x1, waiting for transfers between devices, shards(): lax.all_gather(jnp.sum(lifted * lifted, axis=0), 'fac')  277 us
    dot_general x28, matrix products, contract(): jnp.einsum(pattern, left_side, right_side, precision=precise, preferred_e...  170 us
    all_to_all x1, blocking collectives, shards(): lax.all_to_all(shrunk, 'fac', split_axis=2, concat_axis=0, tiled=True)  96.3 us
    unnamed x64, local copies, waits for them, and re-layouts  23 us
    add x1, other arithmetic, complex_step(): contract(pattern, real_part, matrix[1])  17 us
    reduce_sum x1, other arithmetic, shards(): jnp.sum(lax.all_gather(jnp.sum(lifted * lifted, axis=0), 'fac'), axis=0)  16.9 us
  transfers between devices with their start and end apart: 2, of which 1 were waited for; matrix products, arithmetic and copies ran while one was open for 28% of the time, Pallas kernels for 0%

profile of v1, /device:TPU:0, one launch (start us, length us, event | category | flops | bytes accessed | tf_op | source)
XLA Modules:
  0.0 714.0 jit_solution(6963952747156138731)
XLA Ops:
  7.2 7.4 %all-to-all-start = ((f32[64,96,128]{2,1,0:T(8,128)}), f32[64,96,128]{2,1,0:T(8,128)}, u32[]{:S(2)}, u32[]{:S(2)}) async-start(f32[64,96,128]{2,1,0:T(8,128)} %param.34), calls=%async_computation | async-start | bytes 6291456 | tf_op jit(solution)/shard_map/all_to_all | solution.py:188
  14.7 3.3 copy.165
  18.0 5.8 fusion.127
  23.8 3.6 fusion.126
  27.4 6.6 fusion.35
  34.0 6.8 fusion.37
  40.8 6.6 fusion.60
  47.5 11.3 %fusion.13 = (f32[2,96,64,64]{1,2,3,0:T(8,128)}, f32[2,96,64,64]{1,2,3,0:T(8,128)S(1)}) fusion(f32[2,96,64,64]{1,3,2,0:T(8,128)S(1)} %fusion.60, f32[64,64]{0,1:T(8,128)S(1)} %copy-done.16, f32[64,64]{0,1:T(8,128)S(1)} %copy-done.10, f32[2,96,64,64]{1,3,2,0:T(8,128)S(1)} %fusion.35, f32[64,64,1,1]{0,1,3,2:T(8,128)S(1)} %copy-done.14, ...), kind=kOutput, calls=%fused_computation.20 | convolution fusion | flops 609484800 | bytes 15777792 | tf_op jit(solution)/shard_map/csba,bk->cska/dot_general | solution.py:26
  58.7 7.0 fusion.27
  65.8 7.1 fusion.29
  72.9 5.2 copy.173
  78.1 5.1 copy.178
  83.2 5.3 copy.164
  88.5 9.8 %subtract_bitcast_fusion.1 = f32[2,96,64,64]{1,2,3,0:T(8,128)S(1)} fusion(f32[2,96,64,64]{1,3,2,0:T(8,128)} %fusion.29, f32[64,64,1,1]{0,1,3,2:T(8,128)S(1)} %copy-done.11, f32[2,96,64,64]{1,2,3,0:T(8,128)} %get-tuple-element.4), kind=kOutput, calls=%fused_computation.37 | convolution fusion | flops 604766208 | bytes 9453568 | tf_op jit(solution)/shard_map/cska,aj->csjk/dot_general | solution.py:26
  98.3 6.6 add_bitcast_fusion.1
  104.9 4.4 copy.177
  109.3 4.3 copy.172
  113.7 11.3 %fusion.12 = (f32[2,96,4096]{1,2,0:T(8,128)}, f32[2,96,4096]{1,2,0:T(8,128)}) fusion(f32[2,96,4096]{1,2,0:T(8,128)} %copy.173, f32[2,96,64,64]{1,3,2,0:T(8,128)} %copy.172, s32[2,96,4096]{1,2,0:T(8,128)} %copy.164, f32[2,96,4096]{1,2,0:T(8,128)} %copy.178, f32[2,96,64,64]{1,3,2,0:T(8,128)} %copy.177), kind=kLoop, calls=%fused_computation.17 | loop fusion | flops 3932160 | bytes 22020096 | tf_op jit(solution)/shard_map/mul | solution.py:83
  125.0 10.9 %fusion.19 = f32[2,96,64,64]{1,3,2,0:T(8,128)} fusion(f32[64,64,1,1]{0,1,3,2:T(8,128)S(1)} %copy-done.11, f32[2,96,64,64]{1,3,2,0:T(8,128)} %bitcast.164), kind=kOutput, calls=%fused_computation.38 | convolution fusion | flops 603979776 | bytes 6307840 | tf_op jit(solution)/shard_map/csjk,ja->cska/dot_general | solution.py:26
  135.9 7.1 fusion.21
  143.1 7.1 fusion.23
  150.1 7.2 %fusion.25 = f32[2,96,64,64]{1,3,2,0:T(8,128)} fusion(f32[64,64,1,1]{0,1,3,2:T(8,128)S(1)} %copy-done.11, f32[2,96,64,64]{1,3,2,0:T(8,128)S(1)} %bitcast.163), kind=kOutput, calls=%fused_computation.44 | convolution fusion | flops 603979776 | bytes 6307840 | tf_op jit(solution)/shard_map/csjk,ja->cska/dot_general | solution.py:26
  157.3 17.0 %copy_add_fusion = (f32[2,96,64,64]{1,2,3,0:T(8,128)S(1)}, f32[2,96,64,64]{1,2,3,0:T(8,128)}) fusion(f32[2,96,64,64]{1,3,2,0:T(8,128)} %fusion.19, f32[2,96,64,64]{1,3,2,0:T(8,128)} %fusion.23, f32[2,96,64,64]{1,3,2,0:T(8,128)} %fusion.21, f32[2,96,64,64]{1,3,2,0:T(8,128)} %fusion.25), kind=kLoop, calls=%fused_computation.29 | loop fusion | flops 1572864 | bytes 18874368 | tf_op jit(solution)/shard_map/add | solution.py:59
  174.3 6.7 fusion.74
  181.0 5.5 add_bitcast_fusion
  186.6 6.5 fusion.15
  193.1 5.3 fusion.75
  198.4 5.3 subtract_bitcast_fusion
  203.8 7.4 %fusion.70 = f32[2,64,64,96]{3,2,1,0:T(8,128)} fusion(f32[2,64,64,96]{3,2,1,0:T(8,128)S(1)} %fusion.15, f32[96,96,1,1]{1,0,3,2:T(8,128)S(1)} %copy-done.19, f32[2,96,64,64]{1,2,3,0:T(8,128)S(1)} %subtract_bitcast_fusion), kind=kOutput, calls=%fused_computation.82 | convolution fusion | flops 906756096 | bytes 9474048 | tf_op jit(solution)/shard_map/csba,sr->crba/dot_general | solution.py:26
  211.2 5.3 copy.190
  216.4 5.1 copy.188
  229.0 2.5 fusion.48
  231.9 2.6 pad_maximum_fusion
  234.4 7.8 %copy.189 = f32[2,96,32,134]{3,2,1,0:T(8,128)} copy(f32[2,96,32,134]{1,3,2,0:T(8,128)} %pad_maximum_fusion) | data formatting | bytes 6586368 | tf_op jit(solution)/shard_map/concatenate | solution.py:167
  242.3 8.3 %fusion.128 = f32[2,96,32,128]{3,2,1,0:T(8,128)} fusion(f32[2,96,32,134]{3,2,1,0:T(8,128)} %copy.189, f32[134,128,1,1]{1,0,3,2:T(8,128)S(1)} %copy-done.18), kind=kOutput, calls=%fused_computation.138 | convolution fusion | flops 1264582656 | bytes 6507520 | tf_op jit(solution)/shard_map/...m,mk->...k/dot_general | solution.py:26
  250.5 4.9 reshape.53
  255.5 6.3 fusion.9
  261.8 3.3 fusion.45
  266.6 5.5 fusion
  274.9 8.4 %fusion.43 = f32[2,96,32,64]{1,3,2,0:T(8,128)S(1)} fusion(f32[70,64,1,1]{0,1,3,2:T(8,128)S(1)} %copy-done.23, f32[2,96,32,70]{3,2,1,0:T(8,128)S(1)} %maximum_maximum_fusion), kind=kOutput, calls=%fused_computation.63 | convolution fusion | flops 330301440 | bytes 3311104 | tf_op jit(solution)/shard_map/...m,mk->...k/dot_general | solution.py:26
  286.8 3.1 copy.213
  291.6 5.5 multiply_reduce_fusion
  298.9 276.9 %all-gather.2.cloned.1.call-done = f32[32,96,4096]{2,1,0:T(8,128)} async-done(((f32[1,96,4096]{2,1,0:T(8,128)}), f32[32,96,4096]{2,1,0:T(8,128)}) %all-gather.2.cloned.1.call-update) | async-done | bytes 50331664 | tf_op jit(solution)/shard_map/all_gather | solution.py:200
  575.7 16.9 %reduce_sum.19 = f32[96,4096]{1,0:T(8,128)S(1)} reduce(f32[32,96,4096]{2,1,0:T(8,128)} %all-gather.2.cloned.1.call-done, f32[]{:T(128)} %constant.19.clone.1), dimensions={0}, to_apply=%region_1.2 | reduce | flops 12189696 | bytes 51904516 | tf_op jit(solution)/shard_map/reduce_sum | solution.py:200
  594.3 1.8 copy.195
  596.1 7.8 %copy_divide_fusion = f32[2,96,4096]{1,0,2:T(2,128)S(1)} fusion(f32[2,96,4096]{1,2,0:T(8,128)} %bitcast.169, f32[96,4096]{0,1:T(8,128)S(1)} %copy.195), kind=kLoop, calls=%fused_computation.24 | loop fusion | flops 786432 | bytes 7864320 | tf_op jit(solution)/shard_map/div | solution.py:201
  603.9 96.3 %all_to_all.33 = f32[2,96,4096]{1,0,2:T(2,128)} all-to-all(f32[2,96,4096]{1,0,2:T(2,128)S(1)} %copy_divide_fusion), channel_id=1, replica_groups=mesh['groups'=1,'fac'=32] {'fac'}, dimensions={2} | all-to-all | bytes 6291456 | tf_op jit(solution)/shard_map/all_to_all | solution.py:202
  700.3 6.6 copy.197
  (92 shorter events, 20.4 us)
Async XLA Ops:
  7.2 7.5 %copy-start.6 = (f32[2,96,4096]{2,1,0:T(8,128)S(1)}, f32[2,96,4096]{2,1,0:T(8,128)}, u32[]{:S(2)}) copy-start(f32[2,96,4096]{2,1,0:T(8,128)} %param.30) | copy-start | bytes 9437188
  7.2 209.3 %all-to-all-start = ((f32[64,96,128]{2,1,0:T(8,128)}), f32[64,96,128]{2,1,0:T(8,128)}, u32[]{:S(2)}, u32[]{:S(2)}) async-start(f32[64,96,128]{2,1,0:T(8,128)} %param.34), calls=%async_computation | async-start | bytes 6291456 | tf_op jit(solution)/shard_map/all_to_all | solution.py:188
  14.6 3.4 copy-start.21
  14.6 561.1 %all-gather.2.cloned.1.call-start = ((), (), s32[]{:S(2)}) async-start(), calls=%async_computation.2 | async-start | bytes 51904512 | tf_op jit(solution)/shard_map/all_gather | solution.py:200
  18.0 5.8 copy-start.1
  18.0 5.8 copy-start.22
  23.8 3.6 copy-start.11
  27.4 6.6 copy-start.14
  40.8 6.6 copy-start.10
  40.8 6.6 copy-start.16
  88.4 9.8 %copy-start.3 = (f32[2,96,64,64]{1,2,3,0:T(8,128)S(1)}, f32[2,96,64,64]{1,2,3,0:T(8,128)}, u32[]{:S(2)}) copy-start(f32[2,96,64,64]{1,2,3,0:T(8,128)} %get-tuple-element.4) | copy-start | bytes 9437188
  88.4 9.8 %copy-start.8 = (f32[2,96,64,64]{1,3,2,0:T(8,128)S(1)}, f32[2,96,64,64]{1,3,2,0:T(8,128)}, u32[]{:S(2)}) copy-start(f32[2,96,64,64]{1,3,2,0:T(8,128)} %fusion.27) | copy-start | bytes 9437188
  125.0 10.9 %copy-start.5 = (f32[2,96,4096]{1,2,0:T(8,128)S(1)}, f32[2,96,4096]{1,2,0:T(8,128)}, u32[]{:S(2)}) copy-start(f32[2,96,4096]{1,2,0:T(8,128)} %get-tuple-element.19) | copy-start | bytes 9437188
  125.0 10.9 %copy-start.13 = (f32[64,64,1,1]{0,1,3,2:T(8,128)S(1)}, f32[64,64,1,1]{0,1,3,2:T(8,128)}, u32[]{:S(2)}) copy-start(f32[64,64,1,1]{0,1,3,2:T(8,128)} %constant.74) | copy-start | bytes 49156
  135.9 7.1 copy-start.4
  157.3 17.0 %copy-start.12 = (f32[64,64]{0,1:T(8,128)S(1)}, f32[64,64]{0,1:T(8,128)}, u32[]{:S(2)}) copy-start(f32[64,64]{0,1:T(8,128)} %constant.58.clone) | copy-start | bytes 49156
  174.3 6.7 copy-start
  181.0 5.6 copy-start.20
  198.4 5.4 copy-start.19
  216.4 10.0 %copy-start.28 = (f32[22,16,1,1]{0,1,3,2:T(8,128)S(1)}, f32[22,16,1,1]{0,1,3,2:T(8,128)}, u32[]{:S(2)}) copy-start(f32[22,16,1,1]{0,1,3,2:T(8,128)} %constant.77) | copy-start | bytes 4228
  221.6 5.8 copy-start.27
  223.5 5.5 copy-start.2
  226.4 2.6 copy-start.26
  234.4 7.8 %copy-start.18 = (f32[134,128,1,1]{1,0,3,2:T(8,128)S(1)}, f32[134,128,1,1]{1,0,3,2:T(8,128)}, u32[]{:S(2)}) copy-start(f32[134,128,1,1]{1,0,3,2:T(8,128)} %constant.80) | copy-start | bytes 205828
  250.5 4.9 copy-start.7
  250.5 4.9 copy-start.15
  261.8 3.4 copy-start.9
  265.7 0.9 copy-start.17
  273.8 1.1 copy-start.23
  274.9 9.6 %copy-start.24 = (f32[38,32,1,1]{0,1,3,2:T(8,128)S(1)}, f32[38,32,1,1]{0,1,3,2:T(8,128)}, u32[]{:S(2)}) copy-start(f32[38,32,1,1]{0,1,3,2:T(8,128)} %constant.84) | copy-start | bytes 14596
  285.7 4.2 copy-start.25
Sparse Core Ops, SparseCore 0:
  299.0 276.6 all-gather.1
